TPU v7x, 512 devices: a whole 4x4x16 slice. The times are simulated.
512 devices in a mesh: gz: 16 (over z), gy: 32 (over x, y, core).
Axes of the slice: x: 4, y: 4, z: 16, core: 2. Of those that a mesh axis runs over, the one named last changes fastest.
Arguments:
- tracer: float32 [512, 1024, 128], P('gz', 'gy'), may hold values from 0.1 to 10
- y_speed: float32 [512, 1024, 128], P('gz', 'gy'), may hold values from -0.4 to 0.4
- z_speed: float32 [512, 1024, 128], P('gz', 'gy'), may hold values from -0.4 to 0.4
- kappa: float32 [512, 1024, 128], P('gz', 'gy'), may hold values from 0.5 to 8
Outputs:
- updated: float32 [512, 1024, 128], P('gz', 'gy')
All inputs are finite; a program needn't handle non-finite values.
Results may differ from a plain program's by a relative error of at most 0.0003.
Values sent between devices are 32-bit elements; how exact they have to be, the bound alone decides.
A program may use at most 64 MiB of HBM per device.

v0:
```python
import jax
import jax.numpy as jnp
from jax import lax
from jax.sharding import PartitionSpec as P

NSUB = 4
rate_const = 500.0


def padded_2(x, sides, width):
    for axis, dim in sides:
        peers, length = (lax.axis_size(axis), x.shape[dim])
        up = [(i, (i + 1) % peers) for i in range(peers - 1)]
        down = [(j, i) for i, j in up]
        last = lax.slice_in_dim(x, length - width, length, axis=dim)
        leading = lax.slice_in_dim(x, 0, width, axis=dim)
        before = lax.ppermute(last, axis, up)
        after = lax.ppermute(leading, axis, down)
        x = jnp.concatenate([before, x, after], axis=dim)
    return x


def from_behind(x, axis, by):
    peers = lax.axis_size(axis)
    pairs = [(i, i + by) for i in range(peers) if 0 <= i + by < peers]
    return lax.ppermute(x, axis, pairs)


def advect_once(tracer, y_speed, z_speed):
    face_y = 0.5 * (y_speed[:, 1:] + y_speed[:, :-1])
    flux_y = jnp.maximum(face_y, 0.0) * tracer[:, :-1] + jnp.minimum(face_y, 0.0) * tracer[:, 1:]
    diff_y = flux_y[:, 1:] - flux_y[:, :-1]
    face_z = 0.5 * (z_speed[1:] + z_speed[:-1])
    flux_z = jnp.maximum(face_z, 0.0) * tracer[:-1] + jnp.minimum(face_z, 0.0) * tracer[1:]
    diff_z = flux_z[1:] - flux_z[:-1]
    return tracer[1:-1, 1:-1] - diff_y[1:-1] - diff_z[:, 1:-1]


def move_down(values, offset, axis, fill):
    count = values.shape[axis]
    kept = lax.slice_in_dim(values, 0, count - offset, axis=axis)
    padding = jnp.full_like(lax.slice_in_dim(values, 0, offset, axis=axis), fill)
    return jnp.concatenate([padding, kept], axis=axis)


def move_up(values, offset, axis, fill):
    count = values.shape[axis]
    kept = lax.slice_in_dim(values, offset, count, axis=axis)
    padding = jnp.full_like(lax.slice_in_dim(values, 0, offset, axis=axis), fill)
    return jnp.concatenate([kept, padding], axis=axis)


def reduce_lines(sub_diag, main_diag, sup_diag, rights, axis):
    count = main_diag.shape[axis]
    offset = 1
    while offset < count:
        factor_low = -sub_diag / move_down(main_diag, offset, axis, 1.0)
        factor_high = -sup_diag / move_up(main_diag, offset, axis, 1.0)
        new_main = (
            main_diag
            + factor_low * move_down(sup_diag, offset, axis, 0.0)
            + factor_high * move_up(sub_diag, offset, axis, 0.0)
        )
        new_sub = factor_low * move_down(sub_diag, offset, axis, 0.0)
        new_sup = factor_high * move_up(sup_diag, offset, axis, 0.0)
        rights = tuple(
            (
                right
                + factor_low * move_down(right, offset, axis, 0.0)
                + factor_high * move_up(right, offset, axis, 0.0)
                for right in rights
            )
        )
        sub_diag, main_diag, sup_diag = (new_sub, new_main, new_sup)
        offset = offset * 2
    return tuple((right / main_diag for right in rights))


def solve_rows(items):
    tracer_part, kappa_part = items
    count = kappa_part.shape[1]
    inner = rate_const * 0.5 * (kappa_part[:, 1:] + kappa_part[:, :-1])
    lower = jnp.concatenate([rate_const * kappa_part[:, :1], inner], axis=1)
    upper = jnp.concatenate([inner, rate_const * kappa_part[:, count - 1 :]], axis=1)
    main_diag = 1.0 + lower + upper
    zero_row = jnp.zeros_like(kappa_part[:, :1])
    sub_diag = jnp.concatenate([zero_row, -inner], axis=1)
    sup_diag = jnp.concatenate([-inner, zero_row], axis=1)
    solved = reduce_lines(sub_diag, main_diag, sup_diag, (tracer_part,), 1)[0]
    return lax.all_to_all(solved, "gy", split_axis=1, concat_axis=0, tiled=True)


def local(tracer, y_speed, z_speed, kappa):
    depth_z, depth_y, band = tracer.shape
    z_index = lax.axis_index("gz")
    z_count = lax.axis_size("gz")
    fields = jnp.stack([y_speed, z_speed, kappa])
    width = 1
    padded = padded_2(fields, (("gz", 1), ("gy", 2)), 1)
    state = tracer
    for step in range(NSUB):
        rimmed = padded_2(state, (("gz", 0), ("gy", 1)), 1)
        state = advect_once(rimmed, padded[0], padded[1])
    kappa_below = padded[2, width - 1 : width, width : width + depth_y]
    kappa_above = padded[2, width + depth_z : width + depth_z + 1, width : width + depth_y]
    lines = solve_rows(
        (
            lax.all_to_all(state, "gy", split_axis=0, concat_axis=1, tiled=True),
            lax.all_to_all(kappa, "gy", split_axis=0, concat_axis=1, tiled=True),
        )
    )
    inner = rate_const * 0.5 * (kappa[1:] + kappa[:-1])
    low_edge = jnp.where(
        z_index == 0, rate_const * kappa[:1], rate_const * 0.5 * (kappa[:1] + kappa_below)
    )
    high_edge = jnp.where(
        z_index == z_count - 1,
        rate_const * kappa[depth_z - 1 :],
        rate_const * 0.5 * (kappa[depth_z - 1 :] + kappa_above),
    )
    lower = jnp.concatenate([low_edge, inner], axis=0)
    upper = jnp.concatenate([inner, high_edge], axis=0)
    main_diag = 1.0 + lower + upper
    inner_count = depth_z - 1
    zero_row = jnp.zeros_like(kappa[:1])
    sub_local = jnp.concatenate([zero_row, -lower[1:inner_count]], axis=0)
    sup_local = jnp.concatenate([-upper[: inner_count - 1], zero_row], axis=0)
    zero_rows = jnp.zeros_like(kappa[: inner_count - 1])
    first_right = jnp.concatenate([lower[:1], zero_rows], axis=0)
    last_right = jnp.concatenate([zero_rows, upper[inner_count - 1 : inner_count]], axis=0)
    base, toward_low, toward_high = reduce_lines(
        sub_local,
        main_diag[:inner_count],
        sup_local,
        (lines[:inner_count], first_right, last_right),
        0,
    )
    following = from_behind(jnp.stack([base[0], toward_low[0], toward_high[0]]), "gz", -1)
    sep_low = lower[depth_z - 1]
    sep_high = upper[depth_z - 1]
    sub_red = jnp.where(z_index == 0, 0.0, -sep_low * toward_low[inner_count - 1])
    diag_red = (
        main_diag[depth_z - 1] - sep_low * toward_high[inner_count - 1] - sep_high * following[1]
    )
    sup_red = -sep_high * following[2]
    rhs_red = lines[depth_z - 1] + sep_low * base[inner_count - 1] + sep_high * following[0]
    equations = jnp.stack([sub_red, diag_red, sup_red, rhs_red])
    collected = lax.all_gather(equations[None], "gz", axis=0, tiled=True)
    values = reduce_lines(collected[:, 0], collected[:, 1], collected[:, 2], (collected[:, 3],), 0)[
        0
    ]
    sep_here = lax.dynamic_index_in_dim(values, z_index, axis=0, keepdims=False)
    previous = lax.dynamic_index_in_dim(values, jnp.maximum(z_index - 1, 0), axis=0, keepdims=False)
    sep_prev = jnp.where(z_index > 0, previous, 0.0)
    interior = base + sep_prev[None] * toward_low + sep_here[None] * toward_high
    return jnp.concatenate([interior, sep_here[None]], axis=0)


def solution(mesh):
    return jax.shard_map(
        local,
        mesh=mesh,
        in_specs=(
            P("gz", "gy", None),
            P("gz", "gy", None),
            P("gz", "gy", None),
            P("gz", "gy", None),
        ),
        out_specs=P("gz", "gy", None),
        check_vma=False,
    )
```

profile of v0, /device:TPU:2, one launch (start us, length us, event | category | flops | bytes accessed | tf_op | source)
XLA Modules:
  0.0 254.8 jit_solution(3350201011597019658)
XLA Ops:
  6.5 0.9 fusion.100
  7.4 3.8 %collective-permute-start.4 = (f32[1,32,128]{2,1,0:T(8,128)S(1)}, f32[1,32,128]{2,1,0:T(8,128)S(1)}, u32[]{:S(2)}, u32[]{:S(2)}) collective-permute-start(f32[1,32,128]{2,1,0:T(8,128)S(1)} %get-tuple-element.204), channel_id=1, source_target_pairs={{0,32},{32,64},{64,96},{96,128},{128,160},{160,192},{192,224},{224... | collective-permute-start | bytes 49160 | tf_op jit(solution)/shard_map/ppermute | solution.py:17
  11.2 0.8 pad_maximum_fusion.14
  12.0 3.8 %collective-permute-start = (f32[3,1,32,128]{3,2,1,0:T(8,128)S(1)}, f32[3,1,32,128]{3,2,1,0:T(8,128)S(1)}, u32[]{:S(2)}, u32[]{:S(2)}) collective-permute-start(f32[3,1,32,128]{3,2,1,0:T(8,128)S(1)} %get-tuple-element.65), channel_id=1, source_target_pairs={{0,32},{32,64},{64,96},{96,128},{128,160},{160,192},{192,224},{224... | collective-permute-start | bytes 147464 | tf_op jit(solution)/shard_map/ppermute | solution.py:17
  15.9 1.3 collective-permute-start.1
  17.2 1.3 collective-permute-start.5
  18.5 4.9 %collective-permute-done.5 = f32[1,32,128]{2,1,0:T(8,128)S(1)} collective-permute-done((f32[1,32,128]{2,1,0:T(8,128)S(1)}, f32[1,32,128]{2,1,0:T(8,128)S(1)}, u32[]{:S(2)}, u32[]{:S(2)}) %collective-permute-start.5) | collective-permute-done | bytes 16416 | tf_op jit(solution)/shard_map/ppermute | solution.py:18
  23.5 1.9 collective-permute-start.6
  25.4 5.8 %collective-permute-start.7 = (f32[34,1,128]{2,1,0:T(1,128)S(1)}, f32[34,1,128]{2,1,0:T(1,128)S(1)}, u32[]{:S(2)}, u32[]{:S(2)}) collective-permute-start(f32[34,1,128]{2,1,0:T(1,128)S(1)} %get-tuple-element.114), channel_id=1, source_target_pairs={{1,0},{2,1},{3,2},{4,3},{5,4},{6,5},{7,6},{8,7},{9,8},{10,9},{11,1... | collective-permute-start | bytes 52232 | tf_op jit(solution)/shard_map/ppermute | solution.py:18
  31.2 1.1 pad_maximum_fusion.11
  32.2 1.9 collective-permute-start.2
  34.2 5.8 %collective-permute-start.3 = (f32[3,34,1,128]{3,2,1,0:T(1,128)S(1)}, f32[3,34,1,128]{3,2,1,0:T(1,128)S(1)}, u32[]{:S(2)}, u32[]{:S(2)}) collective-permute-start(f32[3,34,1,128]{3,2,1,0:T(1,128)S(1)} %get-tuple-element.62), channel_id=1, source_target_pairs={{1,0},{2,1},{3,2},{4,3},{5,4},{6,5},{7,6},{8,7},{9,8},{10,9},{11,1... | collective-permute-start | bytes 156680 | tf_op jit(solution)/shard_map/ppermute | solution.py:18
  40.1 1.6 collective-permute-done.3
  41.7 1.4 pad_maximum_fusion
  44.1 4.9 %collective-permute-start.8 = (f32[1,32,128]{2,1,0:T(8,128)S(1)}, f32[1,32,128]{2,1,0:T(8,128)S(1)}, u32[]{:S(2)}, u32[]{:S(2)}) collective-permute-start(f32[1,32,128]{2,1,0:T(8,128)S(1)} %get-tuple-element.201), channel_id=1, source_target_pairs={{0,32},{32,64},{64,96},{96,128},{128,160},{160,192},{192,224},{224... | collective-permute-start | bytes 49160 | tf_op jit(solution)/shard_map/ppermute | solution.py:17
  49.1 1.3 collective-permute-start.9
  50.4 7.8 %all-to-all-start.1 = ((f32[32,32,128]{2,1,0:T(8,128)}), f32[32,32,128]{2,1,0:T(8,128)S(1)}, u32[]{:S(2)}, u32[]{:S(2)}) async-start(f32[32,32,128]{2,1,0:T(8,128)} %param.7), calls=%async_computation.1 | async-start | bytes 1048576 | tf_op jit(solution)/shard_map/all_to_all | solution.py:109
  58.2 2.0 collective-permute-start.10
  60.3 5.6 %collective-permute-start.11 = (f32[34,1,128]{2,1,0:T(1,128)S(1)}, f32[34,1,128]{2,1,0:T(1,128)S(1)}, u32[]{:S(2)}, u32[]{:S(2)}) collective-permute-start(f32[34,1,128]{2,1,0:T(1,128)S(1)} %get-tuple-element.112), channel_id=1, source_target_pairs={{1,0},{2,1},{3,2},{4,3},{5,4},{6,5},{7,6},{8,7},{9,8},{10,9},{11,1... | collective-permute-start | bytes 52232 | tf_op jit(solution)/shard_map/ppermute | solution.py:18
  65.9 1.3 add_multiply_fusion
  67.2 0.4 collective-permute-done.10
  68.6 4.6 %collective-permute-start.12 = (f32[1,32,128]{2,1,0:T(8,128)S(1)}, f32[1,32,128]{2,1,0:T(8,128)S(1)}, u32[]{:S(2)}, u32[]{:S(2)}) collective-permute-start(f32[1,32,128]{2,1,0:T(8,128)S(1)} %get-tuple-element.199), channel_id=1, source_target_pairs={{0,32},{32,64},{64,96},{96,128},{128,160},{160,192},{192,224},{224... | collective-permute-start | bytes 49160 | tf_op jit(solution)/shard_map/ppermute | solution.py:17
  73.1 1.3 collective-permute-start.13
  74.5 5.4 %collective-permute-done.13 = f32[1,32,128]{2,1,0:T(8,128)S(1)} collective-permute-done((f32[1,32,128]{2,1,0:T(8,128)S(1)}, f32[1,32,128]{2,1,0:T(8,128)S(1)}, u32[]{:S(2)}, u32[]{:S(2)}) %collective-permute-start.13) | collective-permute-done | bytes 16416 | tf_op jit(solution)/shard_map/ppermute | solution.py:18
  80.0 1.9 collective-permute-start.14
  81.9 5.8 %collective-permute-start.15 = (f32[34,1,128]{2,1,0:T(1,128)S(1)}, f32[34,1,128]{2,1,0:T(1,128)S(1)}, u32[]{:S(2)}, u32[]{:S(2)}) collective-permute-start(f32[34,1,128]{2,1,0:T(1,128)S(1)} %get-tuple-element.110), channel_id=1, source_target_pairs={{1,0},{2,1},{3,2},{4,3},{5,4},{6,5},{7,6},{8,7},{9,8},{10,9},{11,1... | collective-permute-start | bytes 52232 | tf_op jit(solution)/shard_map/ppermute | solution.py:18
  87.7 1.1 pad_slice_fusion.2
  90.0 3.9 %collective-permute-start.16 = (f32[1,32,128]{2,1,0:T(8,128)S(1)}, f32[1,32,128]{2,1,0:T(8,128)S(1)}, u32[]{:S(2)}, u32[]{:S(2)}) collective-permute-start(f32[1,32,128]{2,1,0:T(8,128)S(1)} %get-tuple-element.197), channel_id=1, source_target_pairs={{0,32},{32,64},{64,96},{96,128},{128,160},{160,192},{192,224},{224... | collective-permute-start | bytes 49160 | tf_op jit(solution)/shard_map/ppermute | solution.py:17
  93.9 1.3 collective-permute-start.17
  95.2 0.8 pad_slice_fusion
  96.1 4.3 %collective-permute-done.17 = f32[1,32,128]{2,1,0:T(8,128)S(1)} collective-permute-done((f32[1,32,128]{2,1,0:T(8,128)S(1)}, f32[1,32,128]{2,1,0:T(8,128)S(1)}, u32[]{:S(2)}, u32[]{:S(2)}) %collective-permute-start.17) | collective-permute-done | bytes 16416 | tf_op jit(solution)/shard_map/ppermute | solution.py:18
  100.4 1.9 collective-permute-start.18
  102.4 5.8 %collective-permute-start.19 = (f32[34,1,128]{2,1,0:T(1,128)S(1)}, f32[34,1,128]{2,1,0:T(1,128)S(1)}, u32[]{:S(2)}, u32[]{:S(2)}) collective-permute-start(f32[34,1,128]{2,1,0:T(1,128)S(1)} %get-tuple-element.108), channel_id=1, source_target_pairs={{1,0},{2,1},{3,2},{4,3},{5,4},{6,5},{7,6},{8,7},{9,8},{10,9},{11,1... | collective-permute-start | bytes 52232 | tf_op jit(solution)/shard_map/ppermute | solution.py:18
  108.1 0.7 fusion.46
  108.9 0.7 collective-permute-done.19
  110.2 1.1 fusion.11
  111.3 8.0 %all-to-all-start = ((f32[32,32,128]{2,1,0:T(8,128)}), f32[32,32,128]{2,1,0:T(8,128)S(1)}, u32[]{:S(2)}, u32[]{:S(2)}) async-start(f32[32,32,128]{2,1,0:T(8,128)} %fusion.11), calls=%async_computation | async-start | bytes 1048576 | tf_op jit(solution)/shard_map/all_to_all | solution.py:108
  119.5 1.1 pad_slice_fusion.5
  120.7 8.5 %all-to-all-done = f32[32,32,128]{2,1,0:T(8,128)S(1)} async-done(((f32[32,32,128]{2,1,0:T(8,128)}), f32[32,32,128]{2,1,0:T(8,128)S(1)}, u32[]{:S(2)}, u32[]{:S(2)}) %all-to-all-start) | async-done | bytes 524320 | tf_op jit(solution)/shard_map/all_to_all | solution.py:108
  129.2 0.4 multiply_add_fusion.16
  129.8 0.9 copy-done.8
  130.8 0.5 multiply_add_fusion.15
  131.9 0.5 multiply_add_fusion.13
  132.9 0.4 multiply_add_fusion.11
  133.9 0.5 multiply_add_fusion.9
  135.0 0.5 multiply_add_fusion.7
  138.4 1.0 add_divide_fusion
  139.4 5.4 %all-to-all-start.2 = ((f32[1,1024,128]{2,0,1:T(1,128)}), f32[1,1024,128]{2,0,1:T(1,128)S(1)}, u32[]{:S(2)}, u32[]{:S(2)}) async-start(f32[1,1024,128]{2,0,1:T(1,128)} %bitcast.8), calls=%async_computation.2 | async-start | bytes 1048576 | tf_op jit(solution)/shard_map/all_to_all | solution.py:90
  145.2 0.9 fusion.60
  146.1 8.5 %all-to-all-done.2 = f32[1,1024,128]{2,0,1:T(1,128)S(1)} async-done(((f32[1,1024,128]{2,0,1:T(1,128)}), f32[1,1024,128]{2,0,1:T(1,128)S(1)}, u32[]{:S(2)}, u32[]{:S(2)}) %all-to-all-start.2) | async-done | bytes 524320 | tf_op jit(solution)/shard_map/all_to_all | solution.py:90
  154.7 0.9 copy-done.13
  156.5 0.8 copy-done.10
  157.6 0.7 multiply_add_fusion.31
  159.2 0.9 multiply_add_fusion.29
  161.0 0.8 multiply_add_fusion.27
  162.2 0.7 multiply_add_fusion.22
  163.0 0.5 add_divide_fusion.3
  164.1 1.3 collective-permute-start.20
  165.4 6.4 %collective-permute-done.20 = f32[3,32,128]{2,1,0:T(8,128)S(1)} collective-permute-done((f32[3,32,128]{2,1,0:T(8,128)S(1)}, f32[3,32,128]{2,1,0:T(8,128)S(1)}, u32[]{:S(2)}, u32[]{:S(2)}) %collective-permute-start.20) | collective-permute-done | bytes 49184 | tf_op jit(solution)/shard_map/ppermute | solution.py:26
  171.8 0.6 pad_maximum_fusion.6
  172.5 69.8 %all-gather.3.cloned.1.call-done = f32[64,32,128]{2,1,0:T(8,128)} async-done(((f32[4,32,128]{2,1,0:T(8,128)}), f32[64,32,128]{2,1,0:T(8,128)}) %all-gather.3.cloned.1.call-update) | async-done | bytes 1048592 | tf_op jit(solution)/shard_map/all_gather | solution.py:148
  242.3 1.9 slice_bitcast_fusion.11
  246.3 0.7 copy-done.7
  247.2 0.8 pad_maximum_fusion.5
  (187 shorter events, 15.9 us)
Async XLA Ops:
  6.5 11.9 %copy-start.5 = (f32[32,32,128]{2,1,0:T(8,128)S(1)}, f32[32,32,128]{2,1,0:T(8,128)}, u32[]{:S(2)}) copy-start(f32[32,32,128]{2,1,0:T(8,128)} %param.4) | copy-start | bytes 1572868
  6.5 24.6 %copy-start.2 = (f32[32,32,128]{2,1,0:T(8,128)S(1)}, f32[32,32,128]{2,1,0:T(8,128)}, u32[]{:S(2)}) copy-start(f32[32,32,128]{2,1,0:T(8,128)} %param.5) | copy-start | bytes 1572868
  6.5 24.6 %copy-start.1 = (f32[32,32,128]{2,1,0:T(8,128)S(1)}, f32[32,32,128]{2,1,0:T(8,128)}, u32[]{:S(2)}) copy-start(f32[32,32,128]{2,1,0:T(8,128)} %param.6) | copy-start | bytes 1572868
  7.4 11.1 %collective-permute-start.4 = (f32[1,32,128]{2,1,0:T(8,128)S(1)}, f32[1,32,128]{2,1,0:T(8,128)S(1)}, u32[]{:S(2)}, u32[]{:S(2)}) collective-permute-start(f32[1,32,128]{2,1,0:T(8,128)S(1)} %get-tuple-element.204), channel_id=1, source_target_pairs={{0,32},{32,64},{64,96},{96,128},{128,160},{160,192},{192,224},{224... | collective-permute-start | bytes 49160 | tf_op jit(solution)/shard_map/ppermute | solution.py:17
  12.0 19.1 %collective-permute-start = (f32[3,1,32,128]{3,2,1,0:T(8,128)S(1)}, f32[3,1,32,128]{3,2,1,0:T(8,128)S(1)}, u32[]{:S(2)}, u32[]{:S(2)}) collective-permute-start(f32[3,1,32,128]{3,2,1,0:T(8,128)S(1)} %get-tuple-element.65), channel_id=1, source_target_pairs={{0,32},{32,64},{64,96},{96,128},{128,160},{160,192},{192,224},{224... | collective-permute-start | bytes 147464 | tf_op jit(solution)/shard_map/ppermute | solution.py:17
  15.9 15.3 %collective-permute-start.1 = (f32[3,1,32,128]{3,2,1,0:T(8,128)S(1)}, f32[3,1,32,128]{3,2,1,0:T(8,128)S(1)}, u32[]{:S(2)}, u32[]{:S(2)}) collective-permute-start(f32[3,1,32,128]{3,2,1,0:T(8,128)S(1)} %get-tuple-element.66), channel_id=1, source_target_pairs={{32,0},{64,32},{96,64},{128,96},{160,128},{192,160},{224,192},{256... | collective-permute-start | bytes 147464 | tf_op jit(solution)/shard_map/ppermute | solution.py:18
  17.2 6.3 %collective-permute-start.5 = (f32[1,32,128]{2,1,0:T(8,128)S(1)}, f32[1,32,128]{2,1,0:T(8,128)S(1)}, u32[]{:S(2)}, u32[]{:S(2)}) collective-permute-start(f32[1,32,128]{2,1,0:T(8,128)S(1)} %get-tuple-element.203), channel_id=1, source_target_pairs={{32,0},{64,32},{96,64},{128,96},{160,128},{192,160},{224,192},{256... | collective-permute-start | bytes 49160 | tf_op jit(solution)/shard_map/ppermute | solution.py:18
  23.5 16.5 %collective-permute-start.6 = (f32[34,1,128]{2,1,0:T(1,128)S(1)}, f32[34,1,128]{2,1,0:T(1,128)S(1)}, u32[]{:S(2)}, u32[]{:S(2)}) collective-permute-start(f32[34,1,128]{2,1,0:T(1,128)S(1)} %get-tuple-element.113), channel_id=1, source_target_pairs={{0,1},{1,2},{2,3},{3,4},{4,5},{5,6},{6,7},{7,8},{8,9},{9,10},{10,1... | collective-permute-start | bytes 52232 | tf_op jit(solution)/shard_map/ppermute | solution.py:17
  25.4 14.6 %collective-permute-start.7 = (f32[34,1,128]{2,1,0:T(1,128)S(1)}, f32[34,1,128]{2,1,0:T(1,128)S(1)}, u32[]{:S(2)}, u32[]{:S(2)}) collective-permute-start(f32[34,1,128]{2,1,0:T(1,128)S(1)} %get-tuple-element.114), channel_id=1, source_target_pairs={{1,0},{2,1},{3,2},{4,3},{5,4},{6,5},{7,6},{8,7},{9,8},{10,9},{11,1... | collective-permute-start | bytes 52232 | tf_op jit(solution)/shard_map/ppermute | solution.py:18
  32.2 7.8 %collective-permute-start.2 = (f32[3,34,1,128]{3,2,1,0:T(1,128)S(1)}, f32[3,34,1,128]{3,2,1,0:T(1,128)S(1)}, u32[]{:S(2)}, u32[]{:S(2)}) collective-permute-start(f32[3,34,1,128]{3,2,1,0:T(1,128)S(1)} %get-tuple-element.61), channel_id=1, source_target_pairs={{0,1},{1,2},{2,3},{3,4},{4,5},{5,6},{6,7},{7,8},{8,9},{9,10},{10,1... | collective-permute-start | bytes 156680 | tf_op jit(solution)/shard_map/ppermute | solution.py:17
  34.2 7.5 %collective-permute-start.3 = (f32[3,34,1,128]{3,2,1,0:T(1,128)S(1)}, f32[3,34,1,128]{3,2,1,0:T(1,128)S(1)}, u32[]{:S(2)}, u32[]{:S(2)}) collective-permute-start(f32[3,34,1,128]{3,2,1,0:T(1,128)S(1)} %get-tuple-element.62), channel_id=1, source_target_pairs={{1,0},{2,1},{3,2},{4,3},{5,4},{6,5},{7,6},{8,7},{9,8},{10,9},{11,1... | collective-permute-start | bytes 156680 | tf_op jit(solution)/shard_map/ppermute | solution.py:18
  44.1 14.0 %collective-permute-start.8 = (f32[1,32,128]{2,1,0:T(8,128)S(1)}, f32[1,32,128]{2,1,0:T(8,128)S(1)}, u32[]{:S(2)}, u32[]{:S(2)}) collective-permute-start(f32[1,32,128]{2,1,0:T(8,128)S(1)} %get-tuple-element.201), channel_id=1, source_target_pairs={{0,32},{32,64},{64,96},{96,128},{128,160},{160,192},{192,224},{224... | collective-permute-start | bytes 49160 | tf_op jit(solution)/shard_map/ppermute | solution.py:17
  49.1 9.1 %collective-permute-start.9 = (f32[1,32,128]{2,1,0:T(8,128)S(1)}, f32[1,32,128]{2,1,0:T(8,128)S(1)}, u32[]{:S(2)}, u32[]{:S(2)}) collective-permute-start(f32[1,32,128]{2,1,0:T(8,128)S(1)} %get-tuple-element.202), channel_id=1, source_target_pairs={{32,0},{64,32},{96,64},{128,96},{160,128},{192,160},{224,192},{256... | collective-permute-start | bytes 49160 | tf_op jit(solution)/shard_map/ppermute | solution.py:18
  50.4 60.9 %all-to-all-start.1 = ((f32[32,32,128]{2,1,0:T(8,128)}), f32[32,32,128]{2,1,0:T(8,128)S(1)}, u32[]{:S(2)}, u32[]{:S(2)}) async-start(f32[32,32,128]{2,1,0:T(8,128)} %param.7), calls=%async_computation.1 | async-start | bytes 1048576 | tf_op jit(solution)/shard_map/all_to_all | solution.py:109
  58.2 9.4 %collective-permute-start.10 = (f32[34,1,128]{2,1,0:T(1,128)S(1)}, f32[34,1,128]{2,1,0:T(1,128)S(1)}, u32[]{:S(2)}, u32[]{:S(2)}) collective-permute-start(f32[34,1,128]{2,1,0:T(1,128)S(1)} %get-tuple-element.111), channel_id=1, source_target_pairs={{0,1},{1,2},{2,3},{3,4},{4,5},{5,6},{6,7},{7,8},{8,9},{9,10},{10,1... | collective-permute-start | bytes 52232 | tf_op jit(solution)/shard_map/ppermute | solution.py:17
  60.3 7.4 %collective-permute-start.11 = (f32[34,1,128]{2,1,0:T(1,128)S(1)}, f32[34,1,128]{2,1,0:T(1,128)S(1)}, u32[]{:S(2)}, u32[]{:S(2)}) collective-permute-start(f32[34,1,128]{2,1,0:T(1,128)S(1)} %get-tuple-element.112), channel_id=1, source_target_pairs={{1,0},{2,1},{3,2},{4,3},{5,4},{6,5},{7,6},{8,7},{9,8},{10,9},{11,1... | collective-permute-start | bytes 52232 | tf_op jit(solution)/shard_map/ppermute | solution.py:18
  67.2 21.6 %copy-start.3 = (f32[31,32,128]{2,1,0:T(8,128)}, f32[31,32,128]{2,1,0:T(8,128)S(1)}, u32[]{:S(2)}) copy-start(f32[31,32,128]{2,1,0:T(8,128)S(1)} %add_multiply_fusion) | copy-start | bytes 1523716
  68.6 6.0 %collective-permute-start.12 = (f32[1,32,128]{2,1,0:T(8,128)S(1)}, f32[1,32,128]{2,1,0:T(8,128)S(1)}, u32[]{:S(2)}, u32[]{:S(2)}) collective-permute-start(f32[1,32,128]{2,1,0:T(8,128)S(1)} %get-tuple-element.199), channel_id=1, source_target_pairs={{0,32},{32,64},{64,96},{96,128},{128,160},{160,192},{192,224},{224... | collective-permute-start | bytes 49160 | tf_op jit(solution)/shard_map/ppermute | solution.py:17
  73.1 6.8 %collective-permute-start.13 = (f32[1,32,128]{2,1,0:T(8,128)S(1)}, f32[1,32,128]{2,1,0:T(8,128)S(1)}, u32[]{:S(2)}, u32[]{:S(2)}) collective-permute-start(f32[1,32,128]{2,1,0:T(8,128)S(1)} %get-tuple-element.200), channel_id=1, source_target_pairs={{32,0},{64,32},{96,64},{128,96},{160,128},{192,160},{224,192},{256... | collective-permute-start | bytes 49160 | tf_op jit(solution)/shard_map/ppermute | solution.py:18
  80.0 8.8 %collective-permute-start.14 = (f32[34,1,128]{2,1,0:T(1,128)S(1)}, f32[34,1,128]{2,1,0:T(1,128)S(1)}, u32[]{:S(2)}, u32[]{:S(2)}) collective-permute-start(f32[34,1,128]{2,1,0:T(1,128)S(1)} %get-tuple-element.109), channel_id=1, source_target_pairs={{0,1},{1,2},{2,3},{3,4},{4,5},{5,6},{6,7},{7,8},{8,9},{9,10},{10,1... | collective-permute-start | bytes 52232 | tf_op jit(solution)/shard_map/ppermute | solution.py:17
  81.9 7.2 %collective-permute-start.15 = (f32[34,1,128]{2,1,0:T(1,128)S(1)}, f32[34,1,128]{2,1,0:T(1,128)S(1)}, u32[]{:S(2)}, u32[]{:S(2)}) collective-permute-start(f32[34,1,128]{2,1,0:T(1,128)S(1)} %get-tuple-element.110), channel_id=1, source_target_pairs={{1,0},{2,1},{3,2},{4,3},{5,4},{6,5},{7,6},{8,7},{9,8},{10,9},{11,1... | collective-permute-start | bytes 52232 | tf_op jit(solution)/shard_map/ppermute | solution.py:18
  90.0 6.1 %collective-permute-start.16 = (f32[1,32,128]{2,1,0:T(8,128)S(1)}, f32[1,32,128]{2,1,0:T(8,128)S(1)}, u32[]{:S(2)}, u32[]{:S(2)}) collective-permute-start(f32[1,32,128]{2,1,0:T(8,128)S(1)} %get-tuple-element.197), channel_id=1, source_target_pairs={{0,32},{32,64},{64,96},{96,128},{128,160},{160,192},{192,224},{224... | collective-permute-start | bytes 49160 | tf_op jit(solution)/shard_map/ppermute | solution.py:17
  93.9 6.5 %collective-permute-start.17 = (f32[1,32,128]{2,1,0:T(8,128)S(1)}, f32[1,32,128]{2,1,0:T(8,128)S(1)}, u32[]{:S(2)}, u32[]{:S(2)}) collective-permute-start(f32[1,32,128]{2,1,0:T(8,128)S(1)} %get-tuple-element.198), channel_id=1, source_target_pairs={{32,0},{64,32},{96,64},{128,96},{160,128},{192,160},{224,192},{256... | collective-permute-start | bytes 49160 | tf_op jit(solution)/shard_map/ppermute | solution.py:18
  100.4 8.4 %collective-permute-start.18 = (f32[34,1,128]{2,1,0:T(1,128)S(1)}, f32[34,1,128]{2,1,0:T(1,128)S(1)}, u32[]{:S(2)}, u32[]{:S(2)}) collective-permute-start(f32[34,1,128]{2,1,0:T(1,128)S(1)} %get-tuple-element.107), channel_id=1, source_target_pairs={{0,1},{1,2},{2,3},{3,4},{4,5},{5,6},{6,7},{7,8},{8,9},{9,10},{10,1... | collective-permute-start | bytes 52232 | tf_op jit(solution)/shard_map/ppermute | solution.py:17
  102.4 7.2 %collective-permute-start.19 = (f32[34,1,128]{2,1,0:T(1,128)S(1)}, f32[34,1,128]{2,1,0:T(1,128)S(1)}, u32[]{:S(2)}, u32[]{:S(2)}) collective-permute-start(f32[34,1,128]{2,1,0:T(1,128)S(1)} %get-tuple-element.108), channel_id=1, source_target_pairs={{1,0},{2,1},{3,2},{4,3},{5,4},{6,5},{7,6},{8,7},{9,8},{10,9},{11,1... | collective-permute-start | bytes 52232 | tf_op jit(solution)/shard_map/ppermute | solution.py:18
  111.3 17.8 %all-to-all-start = ((f32[32,32,128]{2,1,0:T(8,128)}), f32[32,32,128]{2,1,0:T(8,128)S(1)}, u32[]{:S(2)}, u32[]{:S(2)}) async-start(f32[32,32,128]{2,1,0:T(8,128)} %fusion.11), calls=%async_computation | async-start | bytes 1048576 | tf_op jit(solution)/shard_map/all_to_all | solution.py:108
  129.6 1.0 copy-start.8
  129.6 1.2 copy-start.9
  138.3 6.8 %copy-start.4 = (f32[31,32,128]{2,1,0:T(8,128)S(1)}, f32[31,32,128]{2,1,0:T(8,128)}, u32[]{:S(2)}) copy-start(f32[31,32,128]{2,1,0:T(8,128)} %copy-done.3) | copy-start | bytes 1523716
  139.4 15.2 %all-to-all-start.2 = ((f32[1,1024,128]{2,0,1:T(1,128)}), f32[1,1024,128]{2,0,1:T(1,128)S(1)}, u32[]{:S(2)}, u32[]{:S(2)}) async-start(f32[1,1024,128]{2,0,1:T(1,128)} %bitcast.8), calls=%async_computation.2 | async-start | bytes 1048576 | tf_op jit(solution)/shard_map/all_to_all | solution.py:90
  144.8 97.5 %all-gather.3.cloned.1.call-start = ((), (), s32[]{:S(2)}) async-start(), calls=%async_computation.3 | async-start | bytes 1114112 | tf_op jit(solution)/shard_map/all_gather | solution.py:148
  154.6 1.0 copy-start.13
  156.2 1.0 copy-start.10
  156.2 1.2 copy-start.11
  156.3 1.3 copy-start.12
  163.6 8.2 %copy-start.6 = (f32[31,32,128]{2,1,0:T(8,128)}, f32[31,32,128]{2,1,0:T(8,128)S(1)}, u32[]{:S(2)}) copy-start(f32[31,32,128]{2,1,0:T(8,128)S(1)} %get-tuple-element.60) | copy-start | bytes 1523716
  164.1 7.7 %collective-permute-start.20 = (f32[3,32,128]{2,1,0:T(8,128)S(1)}, f32[3,32,128]{2,1,0:T(8,128)S(1)}, u32[]{:S(2)}, u32[]{:S(2)}) collective-permute-start(f32[3,32,128]{2,1,0:T(8,128)S(1)} %pad_maximum_fusion.15), channel_id=1, source_target_pairs={{32,0},{64,32},{96,64},{128,96},{160,128},{192,160},{224,192},{256... | collective-permute-start | bytes 147464 | tf_op jit(solution)/shard_map/ppermute | solution.py:26
  242.3 2.0 copy-start
  245.9 1.0 copy-start.7
Sparse Core Ops, SparseCore 0:
  172.6 69.6 all-gather.2
where the time goes:
time: 256 us; the launch traced here: 255 us
  waiting for transfers between devices  111 us (43%)
  starting transfers between devices  88.6 us (35%)
  other arithmetic  24.4 us (10%)
  local copies, waits for them, and re-layouts  16.1 us (6%)
  between operations  14.8 us (6%)
    all_gather x1, waiting for transfers between devices, local(): collected = lax.all_gather(equations[None], 'gz', axis=0, tiled=True)  69.8 us
    ppermute x10, starting transfers between devices, padded_2(): after = lax.ppermute(leading, axis, down)  35.1 us
    ppermute x10, starting transfers between devices, padded_2(): before = lax.ppermute(last, axis, up)  30.7 us
    ppermute x10, waiting for transfers between devices, padded_2(): after = lax.ppermute(leading, axis, down)  17.3 us
    all_to_all x1, waiting for transfers between devices, solve_rows(): return lax.all_to_all(solved, 'gy', split_axis=1, concat_axis=0, tiled=True)  8.48 us
    all_to_all x1, waiting for transfers between devices, local(): lax.all_to_all(state, 'gy', split_axis=0, concat_axis=1, tiled=True)  8.45 us
    all_to_all x1, starting transfers between devices, local(): lax.all_to_all(state, 'gy', split_axis=0, concat_axis=1, tiled=True)  8.02 us
    all_to_all x1, starting transfers between devices, local(): lax.all_to_all(kappa, 'gy', split_axis=0, concat_axis=1, tiled=True)  7.77 us
  transfers between devices with their start and end apart: 25, of which 12 were waited for; matrix products, arithmetic and copies ran while one was open for 5% of the time, Pallas kernels for 0%

commit v1 on v0

--- a/solution.py
+++ b/solution.py
@@ -5,6 +5,36 @@
 
 NSUB = 4
 rate_const = 500.0
+
+
+def knots_play(content):
+    comm_axis = "gz"
+    plain = jax.lax.axis_size(comm_axis)
+    arr_now = jax.lax.axis_index(comm_axis)
+    block_next, y, r_now = (plain, arr_now, content.shape[0])
+    in_order = []
+    for s in range(block_next):
+        in_order.append((s, (s + 1) % block_next))
+    blocks_here = []
+    for s in range(block_next):
+        blocks_here.append((s, (s - 1) % block_next))
+    everything = jnp.zeros(
+        (*content.shape[:0], block_next * r_now, *content.shape[1:]), content.dtype
+    )
+    everything = lax.dynamic_update_slice_in_dim(everything, content, y * r_now, axis=0)
+    newest = a_next = content
+    s_next = block_next // 2
+    for u in range(1, s_next + 1):
+        newest = jax.lax.ppermute(newest, comm_axis, in_order)
+        everything = lax.dynamic_update_slice_in_dim(
+            everything, newest, (y - u) % block_next * r_now, axis=0
+        )
+        if u < block_next - s_next:
+            a_next = jax.lax.ppermute(a_next, comm_axis, perm=blocks_here)
+            everything = lax.dynamic_update_slice_in_dim(
+                everything, a_next, (y + u) % block_next * r_now, axis=0
+            )
+    return everything
 
 
 def padded_2(x, sides, width):
@@ -145,7 +175,7 @@
     sup_red = -sep_high * following[2]
     rhs_red = lines[depth_z - 1] + sep_low * base[inner_count - 1] + sep_high * following[0]
     equations = jnp.stack([sub_red, diag_red, sup_red, rhs_red])
-    collected = lax.all_gather(equations[None], "gz", axis=0, tiled=True)
+    collected = knots_play(equations[None])
     values = reduce_lines(collected[:, 0], collected[:, 1], collected[:, 2], (collected[:, 3],), 0)[
         0
     ]

time: 256 us -> 231 us (0.902)
  the two profiles are of different devices: /device:TPU:2 before, /device:TPU:128 now
where the time goes in v1:
time: 231 us; the launch traced here: 229 us
  starting transfers between devices  144 us (62%)
  waiting for transfers between devices  43.9 us (19%)
  other arithmetic  24.5 us (11%)
  local copies, waits for them, and re-layouts  14.9 us (6%)
    ppermute x10, starting transfers between devices, padded_2(): before = lax.ppermute(last, axis, up)  33.2 us
    ppermute x7, starting transfers between devices, knots_play(): a_next = jax.lax.ppermute(a_next, comm_axis, perm=blocks_here)  33.1 us
    ppermute x10, starting transfers between devices, padded_2(): after = lax.ppermute(leading, axis, down)  22.8 us
    ppermute x8, starting transfers between devices, knots_play(): newest = jax.lax.ppermute(newest, comm_axis, in_order)  18.1 us
    all_to_all x1, starting transfers between devices, local(): lax.all_to_all(state, 'gy', split_axis=0, concat_axis=1, tiled=True)  15.4 us
    ppermute x10, waiting for transfers between devices, padded_2(): after = lax.ppermute(leading, axis, down)  14.5 us
    all_to_all x1, starting transfers between devices, local(): lax.all_to_all(kappa, 'gy', split_axis=0, concat_axis=1, tiled=True)  12.5 us
    all_to_all x1, waiting for transfers between devices, solve_rows(): return lax.all_to_all(solved, 'gy', split_axis=1, concat_axis=0, tiled=True)  9.82 us
  transfers between devices with their start and end apart: 39, of which 18 were waited for; matrix products, arithmetic and copies ran while one was open for 5% of the time, Pallas kernels for 0%

profile of v1, /device:TPU:128, one launch (start us, length us, event | category | flops | bytes accessed | tf_op | source)
XLA Modules:
  0.0 229.1 jit_solution(15674321954106391350)
XLA Ops:
  0.0 0.9 fusion.99
  0.9 3.8 %collective-permute-start.4 = (f32[1,32,128]{2,1,0:T(8,128)S(1)}, f32[1,32,128]{2,1,0:T(8,128)S(1)}, u32[]{:S(2)}, u32[]{:S(2)}) collective-permute-start(f32[1,32,128]{2,1,0:T(8,128)S(1)} %get-tuple-element.204), channel_id=1, source_target_pairs={{0,32},{32,64},{64,96},{96,128},{128,160},{160,192},{192,224},{224... | collective-permute-start | bytes 49160 | tf_op jit(solution)/shard_map/ppermute | solution.py:47
  5.5 3.8 %collective-permute-start = (f32[3,1,32,128]{3,2,1,0:T(8,128)S(1)}, f32[3,1,32,128]{3,2,1,0:T(8,128)S(1)}, u32[]{:S(2)}, u32[]{:S(2)}) collective-permute-start(f32[3,1,32,128]{3,2,1,0:T(8,128)S(1)} %get-tuple-element.65), channel_id=1, source_target_pairs={{0,32},{32,64},{64,96},{96,128},{128,160},{160,192},{192,224},{224... | collective-permute-start | bytes 147464 | tf_op jit(solution)/shard_map/ppermute | solution.py:47
  9.3 3.2 %collective-permute-start.1 = (f32[3,1,32,128]{3,2,1,0:T(8,128)S(1)}, f32[3,1,32,128]{3,2,1,0:T(8,128)S(1)}, u32[]{:S(2)}, u32[]{:S(2)}) collective-permute-start(f32[3,1,32,128]{3,2,1,0:T(8,128)S(1)} %get-tuple-element.66), channel_id=1, source_target_pairs={{32,0},{64,32},{96,64},{128,96},{160,128},{192,160},{224,192},{256... | collective-permute-start | bytes 147464 | tf_op jit(solution)/shard_map/ppermute | solution.py:48
  12.6 2.0 collective-permute-start.5
  14.7 3.5 %collective-permute-done.5 = f32[1,32,128]{2,1,0:T(8,128)S(1)} collective-permute-done((f32[1,32,128]{2,1,0:T(8,128)S(1)}, f32[1,32,128]{2,1,0:T(8,128)S(1)}, u32[]{:S(2)}, u32[]{:S(2)}) %collective-permute-start.5) | collective-permute-done | bytes 16416 | tf_op jit(solution)/shard_map/ppermute | solution.py:48
  18.2 1.3 collective-permute-start.6
  19.5 1.3 collective-permute-start.7
  20.9 1.1 pad_maximum_fusion.11
  21.9 4.8 %collective-permute-start.2 = (f32[3,34,1,128]{3,2,1,0:T(1,128)S(1)}, f32[3,34,1,128]{3,2,1,0:T(1,128)S(1)}, u32[]{:S(2)}, u32[]{:S(2)}) collective-permute-start(f32[3,34,1,128]{3,2,1,0:T(1,128)S(1)} %get-tuple-element.61), channel_id=1, source_target_pairs={{0,1},{1,2},{2,3},{3,4},{4,5},{5,6},{6,7},{7,8},{8,9},{9,10},{10,1... | collective-permute-start | bytes 156680 | tf_op jit(solution)/shard_map/ppermute | solution.py:47
  26.8 1.3 collective-permute-start.3
  28.2 2.9 %collective-permute-done.3 = f32[3,34,1,128]{3,2,1,0:T(1,128)S(1)} collective-permute-done((f32[3,34,1,128]{3,2,1,0:T(1,128)S(1)}, f32[3,34,1,128]{3,2,1,0:T(1,128)S(1)}, u32[]{:S(2)}, u32[]{:S(2)}) %collective-permute-start.3) | collective-permute-done | bytes 52256 | tf_op jit(solution)/shard_map/ppermute | solution.py:48
  31.1 1.4 pad_maximum_fusion
  33.6 3.6 %collective-permute-start.8 = (f32[1,32,128]{2,1,0:T(8,128)S(1)}, f32[1,32,128]{2,1,0:T(8,128)S(1)}, u32[]{:S(2)}, u32[]{:S(2)}) collective-permute-start(f32[1,32,128]{2,1,0:T(8,128)S(1)} %get-tuple-element.201), channel_id=1, source_target_pairs={{0,32},{32,64},{64,96},{96,128},{128,160},{160,192},{192,224},{224... | collective-permute-start | bytes 49160 | tf_op jit(solution)/shard_map/ppermute | solution.py:47
  37.2 3.4 %collective-permute-start.9 = (f32[1,32,128]{2,1,0:T(8,128)S(1)}, f32[1,32,128]{2,1,0:T(8,128)S(1)}, u32[]{:S(2)}, u32[]{:S(2)}) collective-permute-start(f32[1,32,128]{2,1,0:T(8,128)S(1)} %get-tuple-element.202), channel_id=1, source_target_pairs={{32,0},{64,32},{96,64},{128,96},{160,128},{192,160},{224,192},{256... | collective-permute-start | bytes 49160 | tf_op jit(solution)/shard_map/ppermute | solution.py:48
  40.7 12.5 %all-to-all-start.1 = ((f32[32,32,128]{2,1,0:T(8,128)}), f32[32,32,128]{2,1,0:T(8,128)S(1)}, u32[]{:S(2)}, u32[]{:S(2)}) async-start(f32[32,32,128]{2,1,0:T(8,128)} %param.7), calls=%async_computation.1 | async-start | bytes 1048576 | tf_op jit(solution)/shard_map/all_to_all | solution.py:139
  53.2 2.2 collective-permute-start.10
  55.4 1.3 collective-permute-start.11
  56.7 1.3 add_multiply_fusion
  58.0 1.6 collective-permute-done.11
  60.6 2.7 %collective-permute-start.12 = (f32[1,32,128]{2,1,0:T(8,128)S(1)}, f32[1,32,128]{2,1,0:T(8,128)S(1)}, u32[]{:S(2)}, u32[]{:S(2)}) collective-permute-start(f32[1,32,128]{2,1,0:T(8,128)S(1)} %get-tuple-element.199), channel_id=1, source_target_pairs={{0,32},{32,64},{64,96},{96,128},{128,160},{160,192},{192,224},{224... | collective-permute-start | bytes 49160 | tf_op jit(solution)/shard_map/ppermute | solution.py:47
  63.3 4.4 %collective-permute-start.13 = (f32[1,32,128]{2,1,0:T(8,128)S(1)}, f32[1,32,128]{2,1,0:T(8,128)S(1)}, u32[]{:S(2)}, u32[]{:S(2)}) collective-permute-start(f32[1,32,128]{2,1,0:T(8,128)S(1)} %get-tuple-element.200), channel_id=1, source_target_pairs={{32,0},{64,32},{96,64},{128,96},{160,128},{192,160},{224,192},{256... | collective-permute-start | bytes 49160 | tf_op jit(solution)/shard_map/ppermute | solution.py:48
  67.7 2.4 %collective-permute-done.13 = f32[1,32,128]{2,1,0:T(8,128)S(1)} collective-permute-done((f32[1,32,128]{2,1,0:T(8,128)S(1)}, f32[1,32,128]{2,1,0:T(8,128)S(1)}, u32[]{:S(2)}, u32[]{:S(2)}) %collective-permute-start.13) | collective-permute-done | bytes 16416 | tf_op jit(solution)/shard_map/ppermute | solution.py:48
  70.1 4.1 %collective-permute-start.14 = (f32[34,1,128]{2,1,0:T(1,128)S(1)}, f32[34,1,128]{2,1,0:T(1,128)S(1)}, u32[]{:S(2)}, u32[]{:S(2)}) collective-permute-start(f32[34,1,128]{2,1,0:T(1,128)S(1)} %get-tuple-element.109), channel_id=1, source_target_pairs={{0,1},{1,2},{2,3},{3,4},{4,5},{5,6},{6,7},{7,8},{8,9},{9,10},{10,1... | collective-permute-start | bytes 52232 | tf_op jit(solution)/shard_map/ppermute | solution.py:47
  74.3 1.3 collective-permute-start.15
  75.6 1.1 pad_slice_fusion.2
  78.3 3.7 %collective-permute-start.16 = (f32[1,32,128]{2,1,0:T(8,128)S(1)}, f32[1,32,128]{2,1,0:T(8,128)S(1)}, u32[]{:S(2)}, u32[]{:S(2)}) collective-permute-start(f32[1,32,128]{2,1,0:T(8,128)S(1)} %get-tuple-element.197), channel_id=1, source_target_pairs={{0,32},{32,64},{64,96},{96,128},{128,160},{160,192},{192,224},{224... | collective-permute-start | bytes 49160 | tf_op jit(solution)/shard_map/ppermute | solution.py:47
  82.0 3.3 %collective-permute-start.17 = (f32[1,32,128]{2,1,0:T(8,128)S(1)}, f32[1,32,128]{2,1,0:T(8,128)S(1)}, u32[]{:S(2)}, u32[]{:S(2)}) collective-permute-start(f32[1,32,128]{2,1,0:T(8,128)S(1)} %get-tuple-element.198), channel_id=1, source_target_pairs={{32,0},{64,32},{96,64},{128,96},{160,128},{192,160},{224,192},{256... | collective-permute-start | bytes 49160 | tf_op jit(solution)/shard_map/ppermute | solution.py:48
  85.3 0.9 pad_slice_fusion
  86.2 1.6 collective-permute-done.17
  87.8 3.0 %collective-permute-start.18 = (f32[34,1,128]{2,1,0:T(1,128)S(1)}, f32[34,1,128]{2,1,0:T(1,128)S(1)}, u32[]{:S(2)}, u32[]{:S(2)}) collective-permute-start(f32[34,1,128]{2,1,0:T(1,128)S(1)} %get-tuple-element.107), channel_id=1, source_target_pairs={{0,1},{1,2},{2,3},{3,4},{4,5},{5,6},{6,7},{7,8},{8,9},{9,10},{10,1... | collective-permute-start | bytes 52232 | tf_op jit(solution)/shard_map/ppermute | solution.py:47
  90.8 1.3 collective-permute-start.19
  92.9 1.8 collective-permute-done.19
  95.3 1.1 fusion.11
  96.4 15.4 %all-to-all-start = ((f32[32,32,128]{2,1,0:T(8,128)}), f32[32,32,128]{2,1,0:T(8,128)S(1)}, u32[]{:S(2)}, u32[]{:S(2)}) async-start(f32[32,32,128]{2,1,0:T(8,128)} %fusion.11), calls=%async_computation | async-start | bytes 1048576 | tf_op jit(solution)/shard_map/all_to_all | solution.py:138
  112.0 1.1 pad_slice_fusion.5
  113.2 9.6 %all-to-all-done = f32[32,32,128]{2,1,0:T(8,128)S(1)} async-done(((f32[32,32,128]{2,1,0:T(8,128)}), f32[32,32,128]{2,1,0:T(8,128)S(1)}, u32[]{:S(2)}, u32[]{:S(2)}) %all-to-all-start) | async-done | bytes 524320 | tf_op jit(solution)/shard_map/all_to_all | solution.py:138
  123.4 0.9 copy-done.7
  132.0 1.0 add_divide_fusion
  133.0 4.4 %all-to-all-start.2 = ((f32[1,1024,128]{2,0,1:T(1,128)}), f32[1,1024,128]{2,0,1:T(1,128)S(1)}, u32[]{:S(2)}, u32[]{:S(2)}) async-start(f32[1,1024,128]{2,0,1:T(1,128)} %bitcast.8), calls=%async_computation.2 | async-start | bytes 1048576 | tf_op jit(solution)/shard_map/all_to_all | solution.py:120
  137.5 0.9 fusion.59
  138.4 9.8 %all-to-all-done.2 = f32[1,1024,128]{2,0,1:T(1,128)S(1)} async-done(((f32[1,1024,128]{2,0,1:T(1,128)}), f32[1,1024,128]{2,0,1:T(1,128)S(1)}, u32[]{:S(2)}, u32[]{:S(2)}) %all-to-all-start.2) | async-done | bytes 524320 | tf_op jit(solution)/shard_map/all_to_all | solution.py:120
  148.4 0.9 copy-done.12
  152.9 0.9 multiply_add_fusion.29
  154.6 0.8 multiply_add_fusion.27
  158.0 4.3 %collective-permute-start.20 = (f32[3,32,128]{2,1,0:T(8,128)S(1)}, f32[3,32,128]{2,1,0:T(8,128)S(1)}, u32[]{:S(2)}, u32[]{:S(2)}) collective-permute-start(f32[3,32,128]{2,1,0:T(8,128)S(1)} %pad_maximum_fusion.15), channel_id=1, source_target_pairs={{32,0},{64,32},{96,64},{128,96},{160,128},{192,160},{224,192},{256... | collective-permute-start | bytes 147464 | tf_op jit(solution)/shard_map/ppermute | solution.py:56
  162.6 2.9 %collective-permute-done.20 = f32[3,32,128]{2,1,0:T(8,128)S(1)} collective-permute-done((f32[3,32,128]{2,1,0:T(8,128)S(1)}, f32[3,32,128]{2,1,0:T(8,128)S(1)}, u32[]{:S(2)}, u32[]{:S(2)}) %collective-permute-start.20) | collective-permute-done | bytes 49184 | tf_op jit(solution)/shard_map/ppermute | solution.py:56
  166.3 3.9 %collective-permute-start.21 = (f32[1,4,32,128]{3,2,1,0:T(8,128)S(1)}, f32[1,4,32,128]{3,2,1,0:T(8,128)S(1)}, u32[]{:S(2)}, u32[]{:S(2)}) collective-permute-start(f32[1,4,32,128]{3,2,1,0:T(8,128)S(1)} %fusion.34), channel_id=1, source_target_pairs={{0,32},{32,64},{64,96},{96,128},{128,160},{160,192},{192,224},{224... | collective-permute-start | bytes 196616 | tf_op jit(solution)/shard_map/ppermute | solution.py:28
  170.2 3.1 %collective-permute-start.22 = (f32[1,4,32,128]{3,2,1,0:T(8,128)S(1)}, f32[1,4,32,128]{3,2,1,0:T(8,128)S(1)}, u32[]{:S(2)}, u32[]{:S(2)}) collective-permute-start(f32[1,4,32,128]{3,2,1,0:T(8,128)S(1)} %fusion.34), channel_id=1, source_target_pairs={{0,480},{32,0},{64,32},{96,64},{128,96},{160,128},{192,160},{224,1... | collective-permute-start | bytes 196616 | tf_op jit(solution)/shard_map/ppermute | solution.py:33
  173.7 2.7 %collective-permute-start.23 = (f32[1,4,32,128]{3,2,1,0:T(8,128)S(1)}, f32[1,4,32,128]{3,2,1,0:T(8,128)S(1)}, u32[]{:S(2)}, u32[]{:S(2)}) collective-permute-start(f32[1,4,32,128]{3,2,1,0:T(8,128)S(1)} %collective-permute-done.21), channel_id=1, source_target_pairs={{0,32},{32,64},{64,96},{96,128},{128,160},{160,192},{192,224},{224... | collective-permute-start | bytes 196616 | tf_op jit(solution)/shard_map/ppermute | solution.py:28
  176.4 4.3 %collective-permute-start.24 = (f32[1,4,32,128]{3,2,1,0:T(8,128)S(1)}, f32[1,4,32,128]{3,2,1,0:T(8,128)S(1)}, u32[]{:S(2)}, u32[]{:S(2)}) collective-permute-start(f32[1,4,32,128]{3,2,1,0:T(8,128)S(1)} %collective-permute-done.22), channel_id=1, source_target_pairs={{0,480},{32,0},{64,32},{96,64},{128,96},{160,128},{192,160},{224,1... | collective-permute-start | bytes 196616 | tf_op jit(solution)/shard_map/ppermute | solution.py:33
  181.0 1.9 collective-permute-start.25
  182.9 5.1 %collective-permute-start.26 = (f32[1,4,32,128]{3,2,1,0:T(8,128)S(1)}, f32[1,4,32,128]{3,2,1,0:T(8,128)S(1)}, u32[]{:S(2)}, u32[]{:S(2)}) collective-permute-start(f32[1,4,32,128]{3,2,1,0:T(8,128)S(1)} %collective-permute-done.24), channel_id=1, source_target_pairs={{0,480},{32,0},{64,32},{96,64},{128,96},{160,128},{192,160},{224,1... | collective-permute-start | bytes 196616 | tf_op jit(solution)/shard_map/ppermute | solution.py:33
  188.4 1.9 collective-permute-start.27
  190.3 5.1 %collective-permute-start.28 = (f32[1,4,32,128]{3,2,1,0:T(8,128)S(1)}, f32[1,4,32,128]{3,2,1,0:T(8,128)S(1)}, u32[]{:S(2)}, u32[]{:S(2)}) collective-permute-start(f32[1,4,32,128]{3,2,1,0:T(8,128)S(1)} %collective-permute-done.26), channel_id=1, source_target_pairs={{0,480},{32,0},{64,32},{96,64},{128,96},{160,128},{192,160},{224,1... | collective-permute-start | bytes 196616 | tf_op jit(solution)/shard_map/ppermute | solution.py:33
  195.7 1.9 collective-permute-start.29
  197.7 5.1 %collective-permute-start.30 = (f32[1,4,32,128]{3,2,1,0:T(8,128)S(1)}, f32[1,4,32,128]{3,2,1,0:T(8,128)S(1)}, u32[]{:S(2)}, u32[]{:S(2)}) collective-permute-start(f32[1,4,32,128]{3,2,1,0:T(8,128)S(1)} %collective-permute-done.28), channel_id=1, source_target_pairs={{0,480},{32,0},{64,32},{96,64},{128,96},{160,128},{192,160},{224,1... | collective-permute-start | bytes 196616 | tf_op jit(solution)/shard_map/ppermute | solution.py:33
  203.1 1.9 collective-permute-start.31
  205.0 5.1 %collective-permute-start.32 = (f32[1,4,32,128]{3,2,1,0:T(8,128)S(1)}, f32[1,4,32,128]{3,2,1,0:T(8,128)S(1)}, u32[]{:S(2)}, u32[]{:S(2)}) collective-permute-start(f32[1,4,32,128]{3,2,1,0:T(8,128)S(1)} %collective-permute-done.30), channel_id=1, source_target_pairs={{0,480},{32,0},{64,32},{96,64},{128,96},{160,128},{192,160},{224,1... | collective-permute-start | bytes 196616 | tf_op jit(solution)/shard_map/ppermute | solution.py:33
  210.5 1.9 collective-permute-start.33
  212.4 5.1 %collective-permute-start.34 = (f32[1,4,32,128]{3,2,1,0:T(8,128)S(1)}, f32[1,4,32,128]{3,2,1,0:T(8,128)S(1)}, u32[]{:S(2)}, u32[]{:S(2)}) collective-permute-start(f32[1,4,32,128]{3,2,1,0:T(8,128)S(1)} %collective-permute-done.32), channel_id=1, source_target_pairs={{0,480},{32,0},{64,32},{96,64},{128,96},{160,128},{192,160},{224,1... | collective-permute-start | bytes 196616 | tf_op jit(solution)/shard_map/ppermute | solution.py:33
  217.8 1.9 collective-permute-start.35
  219.8 5.4 %collective-permute-done.35 = f32[1,4,32,128]{3,2,1,0:T(8,128)S(1)} collective-permute-done((f32[1,4,32,128]{3,2,1,0:T(8,128)S(1)}, f32[1,4,32,128]{3,2,1,0:T(8,128)S(1)}, u32[]{:S(2)}, u32[]{:S(2)}) %collective-permute-start.35) | collective-permute-done | bytes 65568 | tf_op jit(solution)/shard_map/ppermute | solution.py:28
  228.3 0.8 pad_maximum_fusion.5
  (229 shorter events, 26.8 us)
Async XLA Ops:
  0.0 14.6 %copy-start.4 = (f32[32,32,128]{2,1,0:T(8,128)S(1)}, f32[32,32,128]{2,1,0:T(8,128)}, u32[]{:S(2)}) copy-start(f32[32,32,128]{2,1,0:T(8,128)} %param.4) | copy-start | bytes 1572868
  0.0 20.9 %copy-start.1 = (f32[32,32,128]{2,1,0:T(8,128)S(1)}, f32[32,32,128]{2,1,0:T(8,128)}, u32[]{:S(2)}) copy-start(f32[32,32,128]{2,1,0:T(8,128)} %param.5) | copy-start | bytes 1572868
  0.0 20.9 %copy-start = (f32[32,32,128]{2,1,0:T(8,128)S(1)}, f32[32,32,128]{2,1,0:T(8,128)}, u32[]{:S(2)}) copy-start(f32[32,32,128]{2,1,0:T(8,128)} %param.6) | copy-start | bytes 1572868
  0.9 13.7 %collective-permute-start.4 = (f32[1,32,128]{2,1,0:T(8,128)S(1)}, f32[1,32,128]{2,1,0:T(8,128)S(1)}, u32[]{:S(2)}, u32[]{:S(2)}) collective-permute-start(f32[1,32,128]{2,1,0:T(8,128)S(1)} %get-tuple-element.204), channel_id=1, source_target_pairs={{0,32},{32,64},{64,96},{96,128},{128,160},{160,192},{192,224},{224... | collective-permute-start | bytes 49160 | tf_op jit(solution)/shard_map/ppermute | solution.py:47
  5.5 15.3 %collective-permute-start = (f32[3,1,32,128]{3,2,1,0:T(8,128)S(1)}, f32[3,1,32,128]{3,2,1,0:T(8,128)S(1)}, u32[]{:S(2)}, u32[]{:S(2)}) collective-permute-start(f32[3,1,32,128]{3,2,1,0:T(8,128)S(1)} %get-tuple-element.65), channel_id=1, source_target_pairs={{0,32},{32,64},{64,96},{96,128},{128,160},{160,192},{192,224},{224... | collective-permute-start | bytes 147464 | tf_op jit(solution)/shard_map/ppermute | solution.py:47
  9.3 11.5 %collective-permute-start.1 = (f32[3,1,32,128]{3,2,1,0:T(8,128)S(1)}, f32[3,1,32,128]{3,2,1,0:T(8,128)S(1)}, u32[]{:S(2)}, u32[]{:S(2)}) collective-permute-start(f32[3,1,32,128]{3,2,1,0:T(8,128)S(1)} %get-tuple-element.66), channel_id=1, source_target_pairs={{32,0},{64,32},{96,64},{128,96},{160,128},{192,160},{224,192},{256... | collective-permute-start | bytes 147464 | tf_op jit(solution)/shard_map/ppermute | solution.py:48
  12.6 5.6 %collective-permute-start.5 = (f32[1,32,128]{2,1,0:T(8,128)S(1)}, f32[1,32,128]{2,1,0:T(8,128)S(1)}, u32[]{:S(2)}, u32[]{:S(2)}) collective-permute-start(f32[1,32,128]{2,1,0:T(8,128)S(1)} %get-tuple-element.203), channel_id=1, source_target_pairs={{32,0},{64,32},{96,64},{128,96},{160,128},{192,160},{224,192},{256... | collective-permute-start | bytes 49160 | tf_op jit(solution)/shard_map/ppermute | solution.py:48
  18.2 9.9 %collective-permute-start.6 = (f32[34,1,128]{2,1,0:T(1,128)S(1)}, f32[34,1,128]{2,1,0:T(1,128)S(1)}, u32[]{:S(2)}, u32[]{:S(2)}) collective-permute-start(f32[34,1,128]{2,1,0:T(1,128)S(1)} %get-tuple-element.113), channel_id=1, source_target_pairs={{0,1},{1,2},{2,3},{3,4},{4,5},{5,6},{6,7},{7,8},{8,9},{9,10},{10,1... | collective-permute-start | bytes 52232 | tf_op jit(solution)/shard_map/ppermute | solution.py:47
  19.5 8.6 %collective-permute-start.7 = (f32[34,1,128]{2,1,0:T(1,128)S(1)}, f32[34,1,128]{2,1,0:T(1,128)S(1)}, u32[]{:S(2)}, u32[]{:S(2)}) collective-permute-start(f32[34,1,128]{2,1,0:T(1,128)S(1)} %get-tuple-element.114), channel_id=1, source_target_pairs={{1,0},{2,1},{3,2},{4,3},{5,4},{6,5},{7,6},{8,7},{9,8},{10,9},{11,1... | collective-permute-start | bytes 52232 | tf_op jit(solution)/shard_map/ppermute | solution.py:48
  21.9 6.3 %collective-permute-start.2 = (f32[3,34,1,128]{3,2,1,0:T(1,128)S(1)}, f32[3,34,1,128]{3,2,1,0:T(1,128)S(1)}, u32[]{:S(2)}, u32[]{:S(2)}) collective-permute-start(f32[3,34,1,128]{3,2,1,0:T(1,128)S(1)} %get-tuple-element.61), channel_id=1, source_target_pairs={{0,1},{1,2},{2,3},{3,4},{4,5},{5,6},{6,7},{7,8},{8,9},{9,10},{10,1... | collective-permute-start | bytes 156680 | tf_op jit(solution)/shard_map/ppermute | solution.py:47
  26.8 4.4 %collective-permute-start.3 = (f32[3,34,1,128]{3,2,1,0:T(1,128)S(1)}, f32[3,34,1,128]{3,2,1,0:T(1,128)S(1)}, u32[]{:S(2)}, u32[]{:S(2)}) collective-permute-start(f32[3,34,1,128]{3,2,1,0:T(1,128)S(1)} %get-tuple-element.62), channel_id=1, source_target_pairs={{1,0},{2,1},{3,2},{4,3},{5,4},{6,5},{7,6},{8,7},{9,8},{10,9},{11,1... | collective-permute-start | bytes 156680 | tf_op jit(solution)/shard_map/ppermute | solution.py:48
  33.6 19.6 %collective-permute-start.8 = (f32[1,32,128]{2,1,0:T(8,128)S(1)}, f32[1,32,128]{2,1,0:T(8,128)S(1)}, u32[]{:S(2)}, u32[]{:S(2)}) collective-permute-start(f32[1,32,128]{2,1,0:T(8,128)S(1)} %get-tuple-element.201), channel_id=1, source_target_pairs={{0,32},{32,64},{64,96},{96,128},{128,160},{160,192},{192,224},{224... | collective-permute-start | bytes 49160 | tf_op jit(solution)/shard_map/ppermute | solution.py:47
  37.2 16.0 %collective-permute-start.9 = (f32[1,32,128]{2,1,0:T(8,128)S(1)}, f32[1,32,128]{2,1,0:T(8,128)S(1)}, u32[]{:S(2)}, u32[]{:S(2)}) collective-permute-start(f32[1,32,128]{2,1,0:T(8,128)S(1)} %get-tuple-element.202), channel_id=1, source_target_pairs={{32,0},{64,32},{96,64},{128,96},{160,128},{192,160},{224,192},{256... | collective-permute-start | bytes 49160 | tf_op jit(solution)/shard_map/ppermute | solution.py:48
  40.7 55.7 %all-to-all-start.1 = ((f32[32,32,128]{2,1,0:T(8,128)}), f32[32,32,128]{2,1,0:T(8,128)S(1)}, u32[]{:S(2)}, u32[]{:S(2)}) async-start(f32[32,32,128]{2,1,0:T(8,128)} %param.7), calls=%async_computation.1 | async-start | bytes 1048576 | tf_op jit(solution)/shard_map/all_to_all | solution.py:139
  53.2 4.8 %collective-permute-start.10 = (f32[34,1,128]{2,1,0:T(1,128)S(1)}, f32[34,1,128]{2,1,0:T(1,128)S(1)}, u32[]{:S(2)}, u32[]{:S(2)}) collective-permute-start(f32[34,1,128]{2,1,0:T(1,128)S(1)} %get-tuple-element.111), channel_id=1, source_target_pairs={{0,1},{1,2},{2,3},{3,4},{4,5},{5,6},{6,7},{7,8},{8,9},{9,10},{10,1... | collective-permute-start | bytes 52232 | tf_op jit(solution)/shard_map/ppermute | solution.py:47
  55.4 4.2 %collective-permute-start.11 = (f32[34,1,128]{2,1,0:T(1,128)S(1)}, f32[34,1,128]{2,1,0:T(1,128)S(1)}, u32[]{:S(2)}, u32[]{:S(2)}) collective-permute-start(f32[34,1,128]{2,1,0:T(1,128)S(1)} %get-tuple-element.112), channel_id=1, source_target_pairs={{1,0},{2,1},{3,2},{4,3},{5,4},{6,5},{7,6},{8,7},{9,8},{10,9},{11,1... | collective-permute-start | bytes 52232 | tf_op jit(solution)/shard_map/ppermute | solution.py:48
  58.0 18.7 %copy-start.2 = (f32[31,32,128]{2,1,0:T(8,128)}, f32[31,32,128]{2,1,0:T(8,128)S(1)}, u32[]{:S(2)}) copy-start(f32[31,32,128]{2,1,0:T(8,128)S(1)} %add_multiply_fusion) | copy-start | bytes 1523716
  60.6 7.1 %collective-permute-start.12 = (f32[1,32,128]{2,1,0:T(8,128)S(1)}, f32[1,32,128]{2,1,0:T(8,128)S(1)}, u32[]{:S(2)}, u32[]{:S(2)}) collective-permute-start(f32[1,32,128]{2,1,0:T(8,128)S(1)} %get-tuple-element.199), channel_id=1, source_target_pairs={{0,32},{32,64},{64,96},{96,128},{128,160},{160,192},{192,224},{224... | collective-permute-start | bytes 49160 | tf_op jit(solution)/shard_map/ppermute | solution.py:47
  63.3 6.8 %collective-permute-start.13 = (f32[1,32,128]{2,1,0:T(8,128)S(1)}, f32[1,32,128]{2,1,0:T(8,128)S(1)}, u32[]{:S(2)}, u32[]{:S(2)}) collective-permute-start(f32[1,32,128]{2,1,0:T(8,128)S(1)} %get-tuple-element.200), channel_id=1, source_target_pairs={{32,0},{64,32},{96,64},{128,96},{160,128},{192,160},{224,192},{256... | collective-permute-start | bytes 49160 | tf_op jit(solution)/shard_map/ppermute | solution.py:48
  70.1 6.5 %collective-permute-start.14 = (f32[34,1,128]{2,1,0:T(1,128)S(1)}, f32[34,1,128]{2,1,0:T(1,128)S(1)}, u32[]{:S(2)}, u32[]{:S(2)}) collective-permute-start(f32[34,1,128]{2,1,0:T(1,128)S(1)} %get-tuple-element.109), channel_id=1, source_target_pairs={{0,1},{1,2},{2,3},{3,4},{4,5},{5,6},{6,7},{7,8},{8,9},{9,10},{10,1... | collective-permute-start | bytes 52232 | tf_op jit(solution)/shard_map/ppermute | solution.py:47
  74.3 3.1 %collective-permute-start.15 = (f32[34,1,128]{2,1,0:T(1,128)S(1)}, f32[34,1,128]{2,1,0:T(1,128)S(1)}, u32[]{:S(2)}, u32[]{:S(2)}) collective-permute-start(f32[34,1,128]{2,1,0:T(1,128)S(1)} %get-tuple-element.110), channel_id=1, source_target_pairs={{1,0},{2,1},{3,2},{4,3},{5,4},{6,5},{7,6},{8,7},{9,8},{10,9},{11,1... | collective-permute-start | bytes 52232 | tf_op jit(solution)/shard_map/ppermute | solution.py:48
  78.3 7.9 %collective-permute-start.16 = (f32[1,32,128]{2,1,0:T(8,128)S(1)}, f32[1,32,128]{2,1,0:T(8,128)S(1)}, u32[]{:S(2)}, u32[]{:S(2)}) collective-permute-start(f32[1,32,128]{2,1,0:T(8,128)S(1)} %get-tuple-element.197), channel_id=1, source_target_pairs={{0,32},{32,64},{64,96},{96,128},{128,160},{160,192},{192,224},{224... | collective-permute-start | bytes 49160 | tf_op jit(solution)/shard_map/ppermute | solution.py:47
  82.0 5.8 %collective-permute-start.17 = (f32[1,32,128]{2,1,0:T(8,128)S(1)}, f32[1,32,128]{2,1,0:T(8,128)S(1)}, u32[]{:S(2)}, u32[]{:S(2)}) collective-permute-start(f32[1,32,128]{2,1,0:T(8,128)S(1)} %get-tuple-element.198), channel_id=1, source_target_pairs={{32,0},{64,32},{96,64},{128,96},{160,128},{192,160},{224,192},{256... | collective-permute-start | bytes 49160 | tf_op jit(solution)/shard_map/ppermute | solution.py:48
  87.8 5.1 %collective-permute-start.18 = (f32[34,1,128]{2,1,0:T(1,128)S(1)}, f32[34,1,128]{2,1,0:T(1,128)S(1)}, u32[]{:S(2)}, u32[]{:S(2)}) collective-permute-start(f32[34,1,128]{2,1,0:T(1,128)S(1)} %get-tuple-element.107), channel_id=1, source_target_pairs={{0,1},{1,2},{2,3},{3,4},{4,5},{5,6},{6,7},{7,8},{8,9},{9,10},{10,1... | collective-permute-start | bytes 52232 | tf_op jit(solution)/shard_map/ppermute | solution.py:47
  90.8 3.8 %collective-permute-start.19 = (f32[34,1,128]{2,1,0:T(1,128)S(1)}, f32[34,1,128]{2,1,0:T(1,128)S(1)}, u32[]{:S(2)}, u32[]{:S(2)}) collective-permute-start(f32[34,1,128]{2,1,0:T(1,128)S(1)} %get-tuple-element.108), channel_id=1, source_target_pairs={{1,0},{2,1},{3,2},{4,3},{5,4},{6,5},{7,6},{8,7},{9,8},{10,9},{11,1... | collective-permute-start | bytes 52232 | tf_op jit(solution)/shard_map/ppermute | solution.py:48
  96.4 26.3 %all-to-all-start = ((f32[32,32,128]{2,1,0:T(8,128)}), f32[32,32,128]{2,1,0:T(8,128)S(1)}, u32[]{:S(2)}, u32[]{:S(2)}) async-start(f32[32,32,128]{2,1,0:T(8,128)} %fusion.11), calls=%async_computation | async-start | bytes 1048576 | tf_op jit(solution)/shard_map/all_to_all | solution.py:138
  123.2 1.0 copy-start.7
  123.2 1.2 copy-start.8
  132.0 5.5 %copy-start.3 = (f32[31,32,128]{2,1,0:T(8,128)S(1)}, f32[31,32,128]{2,1,0:T(8,128)}, u32[]{:S(2)}) copy-start(f32[31,32,128]{2,1,0:T(8,128)} %copy-done.2) | copy-start | bytes 1523716
  133.0 15.2 %all-to-all-start.2 = ((f32[1,1024,128]{2,0,1:T(1,128)}), f32[1,1024,128]{2,0,1:T(1,128)S(1)}, u32[]{:S(2)}, u32[]{:S(2)}) async-start(f32[1,1024,128]{2,0,1:T(1,128)} %bitcast.8), calls=%async_computation.2 | async-start | bytes 1048576 | tf_op jit(solution)/shard_map/all_to_all | solution.py:120
  148.2 1.0 copy-start.12
  149.9 1.0 copy-start.9
  149.9 1.2 copy-start.10
  149.9 1.3 copy-start.11
  157.2 0.8 copy-start.5
  158.0 7.5 %collective-permute-start.20 = (f32[3,32,128]{2,1,0:T(8,128)S(1)}, f32[3,32,128]{2,1,0:T(8,128)S(1)}, u32[]{:S(2)}, u32[]{:S(2)}) collective-permute-start(f32[3,32,128]{2,1,0:T(8,128)S(1)} %pad_maximum_fusion.15), channel_id=1, source_target_pairs={{32,0},{64,32},{96,64},{128,96},{160,128},{192,160},{224,192},{256... | collective-permute-start | bytes 147464 | tf_op jit(solution)/shard_map/ppermute | solution.py:56
  166.3 7.4 %collective-permute-start.21 = (f32[1,4,32,128]{3,2,1,0:T(8,128)S(1)}, f32[1,4,32,128]{3,2,1,0:T(8,128)S(1)}, u32[]{:S(2)}, u32[]{:S(2)}) collective-permute-start(f32[1,4,32,128]{3,2,1,0:T(8,128)S(1)} %fusion.34), channel_id=1, source_target_pairs={{0,32},{32,64},{64,96},{96,128},{128,160},{160,192},{192,224},{224... | collective-permute-start | bytes 196616 | tf_op jit(solution)/shard_map/ppermute | solution.py:28
  170.2 6.2 %collective-permute-start.22 = (f32[1,4,32,128]{3,2,1,0:T(8,128)S(1)}, f32[1,4,32,128]{3,2,1,0:T(8,128)S(1)}, u32[]{:S(2)}, u32[]{:S(2)}) collective-permute-start(f32[1,4,32,128]{3,2,1,0:T(8,128)S(1)} %fusion.34), channel_id=1, source_target_pairs={{0,480},{32,0},{64,32},{96,64},{128,96},{160,128},{192,160},{224,1... | collective-permute-start | bytes 196616 | tf_op jit(solution)/shard_map/ppermute | solution.py:33
  173.7 7.4 %collective-permute-start.23 = (f32[1,4,32,128]{3,2,1,0:T(8,128)S(1)}, f32[1,4,32,128]{3,2,1,0:T(8,128)S(1)}, u32[]{:S(2)}, u32[]{:S(2)}) collective-permute-start(f32[1,4,32,128]{3,2,1,0:T(8,128)S(1)} %collective-permute-done.21), channel_id=1, source_target_pairs={{0,32},{32,64},{64,96},{96,128},{128,160},{160,192},{192,224},{224... | collective-permute-start | bytes 196616 | tf_op jit(solution)/shard_map/ppermute | solution.py:28
  176.4 6.6 %collective-permute-start.24 = (f32[1,4,32,128]{3,2,1,0:T(8,128)S(1)}, f32[1,4,32,128]{3,2,1,0:T(8,128)S(1)}, u32[]{:S(2)}, u32[]{:S(2)}) collective-permute-start(f32[1,4,32,128]{3,2,1,0:T(8,128)S(1)} %collective-permute-done.22), channel_id=1, source_target_pairs={{0,480},{32,0},{64,32},{96,64},{128,96},{160,128},{192,160},{224,1... | collective-permute-start | bytes 196616 | tf_op jit(solution)/shard_map/ppermute | solution.py:33
  181.0 7.4 %collective-permute-start.25 = (f32[1,4,32,128]{3,2,1,0:T(8,128)S(1)}, f32[1,4,32,128]{3,2,1,0:T(8,128)S(1)}, u32[]{:S(2)}, u32[]{:S(2)}) collective-permute-start(f32[1,4,32,128]{3,2,1,0:T(8,128)S(1)} %collective-permute-done.23), channel_id=1, source_target_pairs={{0,32},{32,64},{64,96},{96,128},{128,160},{160,192},{192,224},{224... | collective-permute-start | bytes 196616 | tf_op jit(solution)/shard_map/ppermute | solution.py:28
  182.9 7.4 %collective-permute-start.26 = (f32[1,4,32,128]{3,2,1,0:T(8,128)S(1)}, f32[1,4,32,128]{3,2,1,0:T(8,128)S(1)}, u32[]{:S(2)}, u32[]{:S(2)}) collective-permute-start(f32[1,4,32,128]{3,2,1,0:T(8,128)S(1)} %collective-permute-done.24), channel_id=1, source_target_pairs={{0,480},{32,0},{64,32},{96,64},{128,96},{160,128},{192,160},{224,1... | collective-permute-start | bytes 196616 | tf_op jit(solution)/shard_map/ppermute | solution.py:33
  188.4 7.4 %collective-permute-start.27 = (f32[1,4,32,128]{3,2,1,0:T(8,128)S(1)}, f32[1,4,32,128]{3,2,1,0:T(8,128)S(1)}, u32[]{:S(2)}, u32[]{:S(2)}) collective-permute-start(f32[1,4,32,128]{3,2,1,0:T(8,128)S(1)} %collective-permute-done.25), channel_id=1, source_target_pairs={{0,32},{32,64},{64,96},{96,128},{128,160},{160,192},{192,224},{224... | collective-permute-start | bytes 196616 | tf_op jit(solution)/shard_map/ppermute | solution.py:28
  190.3 7.4 %collective-permute-start.28 = (f32[1,4,32,128]{3,2,1,0:T(8,128)S(1)}, f32[1,4,32,128]{3,2,1,0:T(8,128)S(1)}, u32[]{:S(2)}, u32[]{:S(2)}) collective-permute-start(f32[1,4,32,128]{3,2,1,0:T(8,128)S(1)} %collective-permute-done.26), channel_id=1, source_target_pairs={{0,480},{32,0},{64,32},{96,64},{128,96},{160,128},{192,160},{224,1... | collective-permute-start | bytes 196616 | tf_op jit(solution)/shard_map/ppermute | solution.py:33
  195.7 7.4 %collective-permute-start.29 = (f32[1,4,32,128]{3,2,1,0:T(8,128)S(1)}, f32[1,4,32,128]{3,2,1,0:T(8,128)S(1)}, u32[]{:S(2)}, u32[]{:S(2)}) collective-permute-start(f32[1,4,32,128]{3,2,1,0:T(8,128)S(1)} %collective-permute-done.27), channel_id=1, source_target_pairs={{0,32},{32,64},{64,96},{96,128},{128,160},{160,192},{192,224},{224... | collective-permute-start | bytes 196616 | tf_op jit(solution)/shard_map/ppermute | solution.py:28
  197.7 7.4 %collective-permute-start.30 = (f32[1,4,32,128]{3,2,1,0:T(8,128)S(1)}, f32[1,4,32,128]{3,2,1,0:T(8,128)S(1)}, u32[]{:S(2)}, u32[]{:S(2)}) collective-permute-start(f32[1,4,32,128]{3,2,1,0:T(8,128)S(1)} %collective-permute-done.28), channel_id=1, source_target_pairs={{0,480},{32,0},{64,32},{96,64},{128,96},{160,128},{192,160},{224,1... | collective-permute-start | bytes 196616 | tf_op jit(solution)/shard_map/ppermute | solution.py:33
  203.1 7.4 %collective-permute-start.31 = (f32[1,4,32,128]{3,2,1,0:T(8,128)S(1)}, f32[1,4,32,128]{3,2,1,0:T(8,128)S(1)}, u32[]{:S(2)}, u32[]{:S(2)}) collective-permute-start(f32[1,4,32,128]{3,2,1,0:T(8,128)S(1)} %collective-permute-done.29), channel_id=1, source_target_pairs={{0,32},{32,64},{64,96},{96,128},{128,160},{160,192},{192,224},{224... | collective-permute-start | bytes 196616 | tf_op jit(solution)/shard_map/ppermute | solution.py:28
  205.0 7.4 %collective-permute-start.32 = (f32[1,4,32,128]{3,2,1,0:T(8,128)S(1)}, f32[1,4,32,128]{3,2,1,0:T(8,128)S(1)}, u32[]{:S(2)}, u32[]{:S(2)}) collective-permute-start(f32[1,4,32,128]{3,2,1,0:T(8,128)S(1)} %collective-permute-done.30), channel_id=1, source_target_pairs={{0,480},{32,0},{64,32},{96,64},{128,96},{160,128},{192,160},{224,1... | collective-permute-start | bytes 196616 | tf_op jit(solution)/shard_map/ppermute | solution.py:33
  210.5 7.4 %collective-permute-start.33 = (f32[1,4,32,128]{3,2,1,0:T(8,128)S(1)}, f32[1,4,32,128]{3,2,1,0:T(8,128)S(1)}, u32[]{:S(2)}, u32[]{:S(2)}) collective-permute-start(f32[1,4,32,128]{3,2,1,0:T(8,128)S(1)} %collective-permute-done.31), channel_id=1, source_target_pairs={{0,32},{32,64},{64,96},{96,128},{128,160},{160,192},{192,224},{224... | collective-permute-start | bytes 196616 | tf_op jit(solution)/shard_map/ppermute | solution.py:28
  212.4 7.4 %collective-permute-start.34 = (f32[1,4,32,128]{3,2,1,0:T(8,128)S(1)}, f32[1,4,32,128]{3,2,1,0:T(8,128)S(1)}, u32[]{:S(2)}, u32[]{:S(2)}) collective-permute-start(f32[1,4,32,128]{3,2,1,0:T(8,128)S(1)} %collective-permute-done.32), channel_id=1, source_target_pairs={{0,480},{32,0},{64,32},{96,64},{128,96},{160,128},{192,160},{224,1... | collective-permute-start | bytes 196616 | tf_op jit(solution)/shard_map/ppermute | solution.py:33
  217.8 7.4 %collective-permute-start.35 = (f32[1,4,32,128]{3,2,1,0:T(8,128)S(1)}, f32[1,4,32,128]{3,2,1,0:T(8,128)S(1)}, u32[]{:S(2)}, u32[]{:S(2)}) collective-permute-start(f32[1,4,32,128]{3,2,1,0:T(8,128)S(1)} %collective-permute-done.33), channel_id=1, source_target_pairs={{0,32},{32,64},{64,96},{96,128},{128,160},{160,192},{192,224},{224... | collective-permute-start | bytes 196616 | tf_op jit(solution)/shard_map/ppermute | solution.py:28
  227.1 1.0 copy-start.6
